TPU v7x, 256 devices: a whole 4x4x8 slice. The times are simulated.
256 devices in a mesh: slab: 16 (over y, x), mode: 16 (over z, core).
Axes of the slice: x: 4, y: 4, z: 8, core: 2. Of those that a mesh axis runs over, the one named last changes fastest.
Arguments:
- tensor: bfloat16 [512, 131072], P('mode', 'slab'), may hold values from -24 to 24, as said below
- start_block: float32 [512, 128], replicated, may hold values from -6 to 6
Outputs:
- basis_rows: float32 [512, 128], P('mode')
- core_coeffs: float32 [131072, 128], P(('slab', 'mode'))
Inputs may be any that keep to these rules, and one draw needn't show every extreme that they name: `tensor`: entries of the unfolding; each is a row factor times a column factor times a bounded random term.
All inputs are finite; a program needn't handle non-finite values.
Results may differ from a plain program's by a relative error of at most 0.0029.
Values may be sent and summed in bfloat16 or wider, within the bound.
A program may use at most 64 MiB of HBM per device.

v0:
```python
import jax
import jax.numpy as jnp
from jax import lax
from jax.sharding import PartitionSpec as P

highest = lax.Precision.HIGHEST
contract_cols = (((1,), (1,)), ((), ()))
contract_rows = (((0,), (0,)), ((), ()))


def orthonormal(image_block):
    small_gram = jnp.dot(image_block.T, image_block, precision=highest)
    factor = jnp.linalg.cholesky(small_gram)
    return lax.linalg.triangular_solve(
        factor, image_block, left_side=False, lower=True, transpose_a=True
    )


def shards(tensor, start_block):
    row_count = tensor.shape[0]
    mode_index = lax.axis_index("mode")
    regrouped = lax.all_to_all(tensor, "mode", split_axis=1, concat_axis=0, tiled=True)
    local_gram = lax.dot_general(
        regrouped, regrouped, contract_cols, preferred_element_type=jnp.float32
    )
    gram_total = lax.psum(local_gram, ("slab", "mode"))
    image_block = jnp.dot(gram_total, start_block, precision=highest)
    basis_full = orthonormal(image_block)
    basis_low = basis_full.astype(jnp.bfloat16)
    basis_rows = lax.dynamic_slice_in_dim(basis_full, mode_index * row_count, row_count, 0)
    core_coeffs = lax.dot_general(
        regrouped, basis_low, contract_rows, preferred_element_type=jnp.float32
    )
    return (basis_rows, core_coeffs)


def solution(mesh):
    placed = (P("mode", "slab"), P())
    return jax.shard_map(
        shards,
        mesh=mesh,
        in_specs=placed,
        out_specs=(P("mode", None), P(("slab", "mode"), None)),
        check_vma=False,
    )
```

profile of v0, /device:TPU:2, one launch (start us, length us, event | category | flops | bytes accessed | tf_op | source)
XLA Modules:
  0.0 326.6 jit_solution(6227881989262356702)
XLA Ops:
  7.2 0.0 copy-start
  7.2 0.0 all-reduce.2.cloned.1.call-start
  7.2 1.1 copy.16
  8.4 24.3 %all_to_all.19 = bf16[32,16,512]{2,0,1:T(8,128)(2,1)S(1)} all-to-all(bf16[32,16,512]{2,0,1:T(8,128)(2,1)S(1)} %bitcast.28), channel_id=1, replica_groups=mesh['slab'=16,'mode'=16] {'mode'}, dimensions={1} | all-to-all | bytes 1048576 | tf_op jit(solution)/shard_map/all_to_all | solution.py:22
  32.7 1.5 fusion.5
  34.2 0.0 all-reduce.2.cloned.1.call-update
  34.2 257.6 %all-reduce.2.cloned.1.call-done = f32[512,512]{1,0:T(8,128)} async-done(((f32[512,512]{1,0:T(8,128)}), f32[512,512]{1,0:T(8,128)}) %all-reduce.2.cloned.1.call-update) | async-done | bytes 1048592 | tf_op jit(solution)/shard_map/psum | solution.py:26
  291.8 0.0 copy-done
  291.9 2.2 fusion.6
  294.1 0.6 fusion.7
  294.7 0.1 copy.12
  294.8 11.7 %cholesky.16 = f32[128,128]{1,0:T(8,128)S(1)} custom-call(f32[128,128]{1,0:T(8,128)S(1)} %fusion.4), custom_call_target="Cholesky" | custom-call | tf_op jit(solution)/shard_map/jit(cholesky)/cholesky | solution.py:13
  306.5 0.6 compare_reduce_fusion
  307.2 0.7 fusion.1
  307.8 9.8 %custom-call.6 = f32[1,128,128]{1,2,0:T(8,128)S(1)} custom-call(f32[1,128,128]{2,1,0:T(8,128)S(1)} %fusion.1), custom_call_target="InvertDiagBlocksLowerTriangular" | custom-call | tf_op jit(solution)/shard_map/triangular_solve | solution.py:14
  317.6 0.4 fusion.2
  318.0 0.3 convolution_bitcast_fusion
  318.3 0.6 constant_dynamic-slice_fusion
  318.9 0.8 copy.13
  (2 shorter events, 0.0 us)
Async XLA Ops:
  7.2 284.7 %copy-start = (f32[512,128]{1,0:T(8,128)S(1)}, f32[512,128]{1,0:T(8,128)}, u32[]{:S(2)}) copy-start(f32[512,128]{1,0:T(8,128)} %param.3) | copy-start | bytes 786436
  7.2 284.7 %all-reduce.2.cloned.1.call-start = ((), (), s32[]{:S(2)}) async-start(), calls=%async_computation.1 | async-start | bytes 2097152 | tf_op jit(solution)/shard_map/psum | solution.py:26
Sparse Core Ops, SparseCore 0:
  34.3 257.4 all-reduce.1
where the time goes:
time: 327 us
  waiting for transfers between devices  258 us (79%)
  blocking collectives  24.3 us (7%)
  other arithmetic  22.9 us (7%)
  between operations  14.1 us (4%)
  matrix products  4.92 us (2%)
    psum x1, waiting for transfers between devices, shards(): gram_total = lax.psum(local_gram, ('slab', 'mode'))  258 us
    all_to_all x1, blocking collectives, shards(): lax.all_to_all(tensor, 'mode', split_axis=1, concat_axis=0, tiled=True)  24.3 us
    another operation x3, other arithmetic, orthonormal(): factor = jnp.linalg.cholesky(small_gram)  12.4 us
    another operation x2, other arithmetic, orthonormal(): lax.linalg.triangular_solve(factor, image_block, left_side=False, lower=T...  10.5 us
  transfers between devices with their start and end apart: 1, of which 1 were waited for; matrix products, arithmetic and copies ran while one was open for 0% of the time, Pallas kernels for 0%

commit v1 on v0

--- a/solution.py
+++ b/solution.py
@@ -23,7 +23,7 @@
     local_gram = lax.dot_general(
         regrouped, regrouped, contract_cols, preferred_element_type=jnp.float32
     )
-    gram_total = lax.psum(local_gram, ("slab", "mode"))
+    gram_total = lax.psum(lax.psum(local_gram, "mode"), "slab")
     image_block = jnp.dot(gram_total, start_block, precision=highest)
     basis_full = orthonormal(image_block)
     basis_low = basis_full.astype(jnp.bfloat16)

time: 327 us -> 281 us (0.86)
  waiting for transfers between devices: 258 us -> 212 us
    psum x1 -> x2, waiting for transfers between devices: 258 us -> 212 us  [shards(): gram_total = lax.psum(lax.psum(local_gram, 'mode'), 'slab')]
  transfers between devices with their start and end apart: 1 -> 2, of which waited for: 1 -> 2; matrix products, arithmetic and copies ran while one was open for 0% -> 0% of each run, Pallas kernels for 0% -> 0%
where the time goes in v1:
time: 281 us
  waiting for transfers between devices  212 us (75%)
  blocking collectives  24.3 us (9%)
  other arithmetic  22.9 us (8%)
  between operations  14.1 us (5%)
  matrix products  4.92 us (2%)
    psum x2, waiting for transfers between devices, shards(): gram_total = lax.psum(lax.psum(local_gram, 'mode'), 'slab')  212 us
    all_to_all x1, blocking collectives, shards(): lax.all_to_all(tensor, 'mode', split_axis=1, concat_axis=0, tiled=True)  24.3 us
    another operation x3, other arithmetic, orthonormal(): factor = jnp.linalg.cholesky(small_gram)  12.4 us
    another operation x2, other arithmetic, orthonormal(): lax.linalg.triangular_solve(factor, image_block, left_side=False, lower=T...  10.5 us
  transfers between devices with their start and end apart: 2, of which 2 were waited for; matrix products, arithmetic and copies ran while one was open for 0% of the time, Pallas kernels for 0%

profile of v1, /device:TPU:2, one launch (start us, length us, event | category | flops | bytes accessed | tf_op | source)
XLA Modules:
  0.0 280.6 jit_solution(5935104680805084658)
XLA Ops:
  7.2 0.0 copy-start
  7.2 0.0 all-reduce.3.cloned.1.call-start
  7.2 1.1 copy.16
  8.4 24.3 %all_to_all.19 = bf16[32,16,512]{2,0,1:T(8,128)(2,1)S(1)} all-to-all(bf16[32,16,512]{2,0,1:T(8,128)(2,1)S(1)} %bitcast.28), channel_id=1, replica_groups=mesh['slab'=16,'mode'=16] {'mode'}, dimensions={1} | all-to-all | bytes 1048576 | tf_op jit(solution)/shard_map/all_to_all | solution.py:22
  32.7 1.5 fusion.5
  34.2 0.0 all-reduce.3.cloned.1.call-update
  34.2 0.0 all-reduce.5.cloned.1.call-start
  34.2 111.1 %all-reduce.3.cloned.1.call-done = f32[512,512]{1,0:T(8,128)} async-done(((f32[512,512]{1,0:T(8,128)}), f32[512,512]{1,0:T(8,128)}) %all-reduce.3.cloned.1.call-update) | async-done | bytes 1048592 | tf_op jit(solution)/shard_map/psum | solution.py:26
  145.4 0.0 all-reduce.5.cloned.1.call-update
  145.4 100.5 %all-reduce.5.cloned.1.call-done = f32[512,512]{1,0:T(8,128)} async-done(((f32[512,512]{1,0:T(8,128)}), f32[512,512]{1,0:T(8,128)}) %all-reduce.5.cloned.1.call-update) | async-done | bytes 1048592 | tf_op jit(solution)/shard_map/psum | solution.py:26
  245.9 0.0 copy-done
  245.9 2.2 fusion.6
  248.1 0.6 fusion.7
  248.7 0.1 copy.12
  248.8 11.7 %cholesky.16 = f32[128,128]{1,0:T(8,128)S(1)} custom-call(f32[128,128]{1,0:T(8,128)S(1)} %fusion.4), custom_call_target="Cholesky" | custom-call | tf_op jit(solution)/shard_map/jit(cholesky)/cholesky | solution.py:13
  260.6 0.6 compare_reduce_fusion
  261.2 0.7 fusion.1
  261.9 9.8 %custom-call.6 = f32[1,128,128]{1,2,0:T(8,128)S(1)} custom-call(f32[1,128,128]{2,1,0:T(8,128)S(1)} %fusion.1), custom_call_target="InvertDiagBlocksLowerTriangular" | custom-call | tf_op jit(solution)/shard_map/triangular_solve | solution.py:14
  271.7 0.4 fusion.2
  272.1 0.3 convolution_bitcast_fusion
  272.3 0.6 constant_dynamic-slice_fusion
  272.9 0.8 copy.13
  (2 shorter events, 0.0 us)
Async XLA Ops:
  7.2 238.7 %copy-start = (f32[512,128]{1,0:T(8,128)S(1)}, f32[512,128]{1,0:T(8,128)}, u32[]{:S(2)}) copy-start(f32[512,128]{1,0:T(8,128)} %param.3) | copy-start | bytes 786436
  7.2 138.2 %all-reduce.3.cloned.1.call-start = ((), (), s32[]{:S(2)}) async-start(), calls=%async_computation.1 | async-start | bytes 2097152 | tf_op jit(solution)/shard_map/psum | solution.py:26
  34.2 211.7 %all-reduce.5.cloned.1.call-start = ((), (), s32[]{:S(2)}) async-start(), calls=%async_computation.2 | async-start | bytes 2097152 | tf_op jit(solution)/shard_map/psum | solution.py:26
Sparse Core Ops, SparseCore 0:
  34.3 110.9 all-reduce.2
  148.6 97.2 all-reduce.4
